TPU v7x, 32 devices: a whole 2x2x4 slice. The times are simulated.
32 devices in a mesh: groups: 2 (over x), mem: 16 (over z, y, core).
Axes of the slice: x: 2, y: 2, z: 4, core: 2. Of those that a mesh axis runs over, the one named last changes fastest.
Arguments:
- mem_key: bfloat16 [128, 128, 128], P(('groups', 'mem')), parts along dimension 0, may hold values from -6 to 6
- value_base: bfloat16 [128, 128, 512], P(('groups', 'mem')), parts along dimension 0, may hold values from -6 to 6
- memory_labels: int32 [128, 128], P(('groups', 'mem')), parts along dimension 0, may hold values from 0 to 7
- valid_counts: int32 [32], P(('groups', 'mem')), parts along dimension 0, may hold values from 128 to 512, as said below
- query_key: bfloat16 [32, 64, 128], P(('groups', 'mem')), parts along dimension 0, may hold values from -96 to 96
- query_value: bfloat16 [32, 64, 512], P(('groups', 'mem')), parts along dimension 0, may hold values from -6 to 6
- object_embed: bfloat16 [8, 512], replicated, may hold values from -6 to 6
- decode_weight: bfloat16 [3, 3, 1024, 256], replicated, may hold values from -0.0625 to 0.0625
- mask_weight: bfloat16 [256, 8], replicated, may hold values from -0.375 to 0.375
Outputs:
- mask_logits: float32 [32, 64, 8], P(('groups', 'mem')), parts along dimension 0
There are 2 independent parts, one for each index of `groups`. A program takes and returns all parts, laid end to end along the dimension named above; an argument that names none is the same for every part. Nothing has to cross between parts.
Inputs may be any that keep to these rules, and one draw needn't show every extreme that they name: `valid_counts`: live positions of each memory block; some block is full and some holds a quarter.
All inputs are finite; a program needn't handle non-finite values.
Results may differ from a plain program's by a relative error of at most 0.0048.
Values may be sent and summed in bfloat16 or wider, within the bound.
No kernel may reach another device: no remote copies, remote signals or barrier semaphores. Data moves between devices by JAX's collectives and lax.ppermute only.
A program may use at most 320 MiB of HBM per device.

v0:
```python
import math
import jax
import jax.numpy as jnp
from jax import lax
from jax.sharding import PartitionSpec as P


def with_halo(block, sides, width):
    for axis, dim in sides:
        count = lax.axis_size(axis)
        forward = [(i, i + 1) for i in range(count - 1)]
        backward = [(target, source) for source, target in forward]
        low = lax.ppermute(
            lax.slice_in_dim(block, block.shape[dim] - width, None, axis=dim), axis, forward
        )
        high = lax.ppermute(lax.slice_in_dim(block, 0, width, axis=dim), axis, backward)
        block = jnp.concatenate([low, block, high], axis=dim)
    return block


def conv_taps(padded, weight, height, width):
    summed = jnp.zeros((height * width, weight.shape[3]), jnp.float32)
    for row_step in range(3):
        for col_step in range(3):
            window = padded[row_step : row_step + height, col_step : col_step + width].reshape(
                height * width, -1
            )
            summed = summed + jnp.dot(
                window, weight[row_step, col_step], preferred_element_type=jnp.float32
            )
    return summed


def shards(
    mem_key,
    value_base,
    memory_labels,
    valid_counts,
    query_key,
    query_value,
    object_embed,
    decode_weight,
    mask_weight,
):
    key_width = mem_key.shape[2]
    val_width = value_base.shape[2]
    keys_local = mem_key.reshape(-1, key_width)
    onehot = (
        memory_labels.reshape(-1)[:, None]
        == jnp.arange(object_embed.shape[0], dtype=jnp.int32)[None, :]
    ).astype(jnp.bfloat16)
    embedded = jnp.dot(onehot, object_embed, preferred_element_type=jnp.float32)
    mem_value = (value_base.reshape(-1, val_width).astype(jnp.float32) + embedded).astype(
        jnp.bfloat16
    )
    queries = lax.all_gather(query_key, "mem", axis=0, tiled=True).reshape(-1, key_width)
    block_size = keys_local.shape[0]
    scores = jnp.dot(queries, keys_local.T, preferred_element_type=jnp.float32) * (
        1.0 / math.sqrt(key_width)
    )
    is_live = (jnp.arange(block_size, dtype=jnp.int32) < valid_counts[0])[None, :]
    scores = jnp.where(is_live, scores, -jnp.inf)
    block_peak = jnp.max(scores, axis=1)
    weights = jnp.where(is_live, jnp.exp(scores - block_peak[:, None]), 0.0).astype(jnp.bfloat16)
    block_mass = jnp.sum(weights.astype(jnp.float32), axis=1)
    block_values = jnp.dot(weights, mem_value, preferred_element_type=jnp.float32)
    query_height = query_value.shape[0]
    query_width = query_value.shape[1]
    owned = query_height * query_width
    largest = lax.pmax(block_peak, "mem")
    rescale = jnp.exp(block_peak - largest)
    scaled_mass = (rescale * block_mass).reshape(-1, query_width)
    scaled_values = (rescale[:, None] * block_values).reshape(-1, query_width, val_width)
    weight_sum, value_sums = (
        lax.psum_scatter(scaled_mass, "mem", scatter_dimension=0, tiled=True),
        lax.psum_scatter(scaled_values, "mem", scatter_dimension=0, tiled=True),
    )
    weight_sum = weight_sum.reshape(owned)
    value_sums = value_sums.reshape(owned, val_width)
    readout = (
        (value_sums / weight_sum[:, None])
        .astype(jnp.bfloat16)
        .reshape(query_height, query_width, val_width)
    )
    joined = jnp.concatenate([readout, query_value], axis=-1)
    bordered = with_halo(joined, (("mem", 0),), 1)
    bordered = jnp.pad(bordered, ((0, 0), (1, 1), (0, 0)))
    hidden = jax.nn.relu(conv_taps(bordered, decode_weight, query_height, query_width)).astype(
        jnp.bfloat16
    )
    logits = jnp.dot(hidden, mask_weight, preferred_element_type=jnp.float32)
    return logits.reshape(query_height, query_width, mask_weight.shape[1])


def solution(mesh):
    placed = (
        P(("groups", "mem"), None, None),
        P(("groups", "mem"), None, None),
        P(("groups", "mem"), None),
        P(("groups", "mem")),
        P(("groups", "mem"), None, None),
        P(("groups", "mem"), None, None),
        P(),
        P(),
        P(),
    )
    return jax.shard_map(
        shards,
        mesh=mesh,
        in_specs=placed,
        out_specs=P(("groups", "mem"), None, None),
        check_vma=False,
    )
```

profile of v0, /device:TPU:5, one launch (start us, length us, event | category | flops | bytes accessed | tf_op | source)
XLA Modules:
  0.0 154.1 jit_solution(16942197713252962668)
XLA Ops:
  6.5 0.0 copy-start
  6.5 0.0 reduce-scatter.2.cloned.1.call-start
  7.2 19.4 %all_gather.3 = bf16[16,64,128]{2,1,0:T(8,128)(2,1)S(1)} all-gather(bf16[1,64,128]{2,1,0:T(8,128)(2,1)} %param.13), channel_id=1, replica_groups=mesh['groups'=2,'mem'=16] {'mem'}, dimensions={0}, use_global_device_ids=true | all-gather | bytes 278528 | tf_op jit(solution)/shard_map/all_gather | solution.py:56
  26.6 0.0 copy-done
  26.6 0.5 fusion
  27.1 0.0 copy-start.3
  27.1 0.0 copy-start.4
  27.1 28.3 %pmax.7 = f32[1024]{0:T(1024)S(1)} all-reduce(f32[1024]{0:T(1024)S(1)} %get-tuple-element.9), channel_id=1, replica_groups=mesh['groups'=2,'mem'=16] {'mem'}, use_global_device_ids=true, to_apply=%region_1.2 | all-reduce | flops 1024 | bytes 8192 | tf_op jit(solution)/shard_map/pmax | solution.py:70
  55.4 0.6 convert_reduce_fusion
  56.0 0.0 copy-done.3
  56.0 0.0 copy-done.4
  56.0 0.0 copy-start.5
  56.0 3.4 %convolution_multiply_fusion = f32[1024,512]{1,0:T(8,128)} fusion(bf16[1024,512]{0,1:T(8,128)(2,1)S(1)} %get-tuple-element.8, bf16[8,512]{1,0:T(8,128)(2,1)S(1)} %copy-done.3, bf16[512,512]{1,0:T(8,128)(2,1)} %bitcast.77, f32[1024]{0:T(1024)S(1)} %get-tuple-element.6, s32[512]{0:T(512)S(1)} %bitcast.78), kind=kOutput, calls=%fused_computation.4 | convolution fusion | flops 542380032 | bytes 3684352 | tf_op jit(solution)/shard_map/dot_general | solution.py:66
  59.4 0.0 copy-start.1
  59.4 0.0 reduce-scatter.2.cloned.1.call-update
  59.5 0.1 reshape.64
  59.5 0.0 copy-done.5
  59.5 0.6 dynamic-slice
  60.1 30.3 %all-reduce.1 = f32[16,64]{1,0:T(8,128)S(1)} all-reduce(f32[16,64]{1,0:T(8,128)S(1)} %reshape.64), channel_id=3, replica_groups=mesh['groups'=2,'mem'=16] {'mem'}, use_global_device_ids=true, to_apply=%region_4.5.clone | all-reduce | flops 1024 | bytes 8192
  90.5 0.7 dynamic-slice_bitcast_fusion
  91.1 30.0 %reduce-scatter.2.cloned.1.call-done = f32[1,64,512]{2,1,0:T(8,128)} async-done(((f32[16,64,512]{2,1,0:T(8,128)}), f32[1,64,512]{2,1,0:T(8,128)}) %reduce-scatter.2.cloned.1.call-update) | async-done | bytes 131088 | tf_op jit(solution)/shard_map/reduce_scatter | solution.py:76
  121.1 1.0 divide_convert_fusion
  122.1 0.0 copy-done.1
  122.1 5.8 %collective-permute-start = (bf16[1,64,1024]{2,1,0:T(8,128)(2,1)S(1)}, bf16[1,64,1024]{2,1,0:T(8,128)(2,1)S(1)}, u32[]{:S(2)}, u32[]{:S(2)}) collective-permute-start(bf16[1,64,1024]{2,1,0:T(8,128)(2,1)S(1)} %pad_maximum_fusion), channel_id=1, source_target_pairs={{0,1},{1,2},{2,3},{3,4},{4,5},{5,6},{6,7},{7,8},{8,9},{9,10},{10,1... | collective-permute-start | bytes 393224 | tf_op jit(solution)/shard_map/ppermute | solution.py:13
  127.9 1.9 %collective-permute-start.1 = (bf16[1,64,1024]{2,1,0:T(8,128)(2,1)S(1)}, bf16[1,64,1024]{2,1,0:T(8,128)(2,1)S(1)}, u32[]{:S(2)}, u32[]{:S(2)}) collective-permute-start(bf16[1,64,1024]{2,1,0:T(8,128)(2,1)S(1)} %pad_maximum_fusion), channel_id=1, source_target_pairs={{1,0},{2,1},{3,2},{4,3},{5,4},{6,5},{7,6},{8,7},{9,8},{10,9},{11,1... | collective-permute-start | bytes 393224 | tf_op jit(solution)/shard_map/ppermute | solution.py:16
  129.8 0.0 collective-permute-done
  129.8 5.2 %collective-permute-done.1 = bf16[1,64,1024]{2,1,0:T(8,128)(2,1)S(1)} collective-permute-done((bf16[1,64,1024]{2,1,0:T(8,128)(2,1)S(1)}, bf16[1,64,1024]{2,1,0:T(8,128)(2,1)S(1)}, u32[]{:S(2)}, u32[]{:S(2)}) %collective-permute-start.1) | collective-permute-done | bytes 131104 | tf_op jit(solution)/shard_map/ppermute | solution.py:16
  135.1 0.1 select_maximum_fusion
  135.2 1.2 fusion.19
  136.5 1.2 fusion.9
  137.7 1.3 convolution_add_fusion.7
  139.0 0.0 copy-start.2
  139.0 1.3 convolution_add_fusion.6
  140.3 1.3 convolution_add_fusion.5
  141.5 1.3 convolution_add_fusion.4
  142.8 1.3 convolution_add_fusion.3
  144.0 1.3 convolution_add_fusion.2
  145.3 0.0 copy-done.2
  145.3 2.0 %fusion.6 = f32[1,64,8]{1,2,0:T(8,128)} fusion(bf16[256,8]{0,1:T(8,128)(2,1)S(1)} %copy-done.2, f32[64,256]{1,0:T(8,128)S(1)} %fusion.9, f32[64,256]{1,0:T(8,128)S(1)} %convolution_add_fusion.2, bf16[3,3,1024,256]{3,2,1,0:T(8,128)(2,1)} %param.16, bf16[1,64,1024]{2,1,0:T(8,128)(2,1)S(1)} %collective-permute-done.1), kind=kOutput, calls=%fused_computation.20 | convolution fusion | flops 33882112 | bytes 792576 | tf_op jit(solution)/shard_map/dot_general | solution.py:91
  (3 shorter events, 0.0 us)
Async XLA Ops:
  6.5 20.1 %copy-start = (bf16[4,128,128]{2,1,0:T(8,128)(2,1)S(1)}, bf16[4,128,128]{2,1,0:T(8,128)(2,1)}, u32[]{:S(2)}) copy-start(bf16[4,128,128]{2,1,0:T(8,128)(2,1)} %param.9) | copy-start | bytes 393220
  6.5 114.5 %reduce-scatter.2.cloned.1.call-start = ((), (), s32[]{:S(2)}) async-start(), calls=%async_computation.1 | async-start | bytes 2228224 | tf_op jit(solution)/shard_map/reduce_scatter | solution.py:76
  27.1 28.9 %copy-start.3 = (bf16[8,512]{1,0:T(8,128)(2,1)S(1)}, bf16[8,512]{1,0:T(8,128)(2,1)}, u32[]{:S(2)}) copy-start(bf16[8,512]{1,0:T(8,128)(2,1)} %param.15) | copy-start | bytes 24580
  27.1 28.9 %copy-start.4 = (s32[4,128]{1,0:T(4,128)S(1)}, s32[4,128]{1,0:T(4,128)}, u32[]{:S(2)}) copy-start(s32[4,128]{1,0:T(4,128)} %param.11) | copy-start | bytes 6148
  56.0 3.5 %copy-start.5 = (u32[32]{0:T(128)S(1)}, u32[32]{0:T(128)}, u32[]{:S(2)}) copy-start(u32[32]{0:T(128)} %constant.21) | copy-start | bytes 388
  59.4 62.6 %copy-start.1 = (bf16[1,64,512]{2,1,0:T(8,128)(2,1)S(1)}, bf16[1,64,512]{2,1,0:T(8,128)(2,1)}, u32[]{:S(2)}) copy-start(bf16[1,64,512]{2,1,0:T(8,128)(2,1)} %param.14) | copy-start | bytes 196612
  122.1 7.7 %collective-permute-start = (bf16[1,64,1024]{2,1,0:T(8,128)(2,1)S(1)}, bf16[1,64,1024]{2,1,0:T(8,128)(2,1)S(1)}, u32[]{:S(2)}, u32[]{:S(2)}) collective-permute-start(bf16[1,64,1024]{2,1,0:T(8,128)(2,1)S(1)} %pad_maximum_fusion), channel_id=1, source_target_pairs={{0,1},{1,2},{2,3},{3,4},{4,5},{5,6},{6,7},{7,8},{8,9},{9,10},{10,1... | collective-permute-start | bytes 393224 | tf_op jit(solution)/shard_map/ppermute | solution.py:13
  127.9 7.2 %collective-permute-start.1 = (bf16[1,64,1024]{2,1,0:T(8,128)(2,1)S(1)}, bf16[1,64,1024]{2,1,0:T(8,128)(2,1)S(1)}, u32[]{:S(2)}, u32[]{:S(2)}) collective-permute-start(bf16[1,64,1024]{2,1,0:T(8,128)(2,1)S(1)} %pad_maximum_fusion), channel_id=1, source_target_pairs={{1,0},{2,1},{3,2},{4,3},{5,4},{6,5},{7,6},{8,7},{9,8},{10,9},{11,1... | collective-permute-start | bytes 393224 | tf_op jit(solution)/shard_map/ppermute | solution.py:16
  139.0 6.3 %copy-start.2 = (bf16[256,8]{0,1:T(8,128)(2,1)S(1)}, bf16[256,8]{0,1:T(8,128)(2,1)}, u32[]{:S(2)}) copy-start(bf16[256,8]{0,1:T(8,128)(2,1)} %param.17) | copy-start | bytes 12292
Sparse Core Ops, SparseCore 0:
  59.6 61.4 reduce-scatter.1
where the time goes:
time: 155 us; the launch traced here: 154 us
  blocking collectives  78 us (50%)
  waiting for transfers between devices  35.2 us (23%)
  matrix products  15.8 us (10%)
  between operations  14.3 us (9%)
  starting transfers between devices  7.7 us (5%)
  other arithmetic  1.72 us (1%)
    unnamed x1, blocking collectives  30.3 us
    reduce_scatter x1, waiting for transfers between devices, shards(): lax.psum_scatter(scaled_values, 'mem', scatter_dimension=0, tiled=True)  30 us
    pmax x1, blocking collectives, shards(): largest = lax.pmax(block_peak, 'mem')  28.3 us
    all_gather x1, blocking collectives, shards(): lax.all_gather(query_key, 'mem', axis=0, tiled=True).reshape(-1, key_width)  19.4 us
    dot_general x8, matrix products, conv_taps(): jnp.dot(window, weight[row_step, col_step], preferred_element_type=jnp.fl...  10 us
    ppermute x1, starting transfers between devices, with_halo(): lax.ppermute(lax.slice_in_dim(block, block.shape[dim] - width, None, axis...  5.78 us
    ppermute x1, waiting for transfers between devices, with_halo(): lax.ppermute(lax.slice_in_dim(block, 0, width, axis=dim), axis, backward)  5.25 us
    dot_general x1, matrix products, shards(): jnp.dot(weights, mem_value, preferred_element_type=jnp.float32)  3.39 us
  transfers between devices with their start and end apart: 3, of which 2 were waited for; matrix products, arithmetic and copies ran while one was open for 1% of the time, Pallas kernels for 0%

commit v1 on v0

--- a/solution.py
+++ b/solution.py
@@ -3,6 +3,18 @@
 import jax.numpy as jnp
 from jax import lax
 from jax.sharding import PartitionSpec as P
+
+
+def gather_by_bits(x, axis, dim):
+    ways, here = (lax.axis_size(axis), lax.axis_index(axis))
+    grown, reach = (x, 1)
+    while reach < ways:
+        theirs = lax.ppermute(grown, axis, [(d, d ^ reach) for d in range(ways)])
+        mine_first = jnp.concatenate([grown, theirs], axis=dim)
+        theirs_first = jnp.concatenate([theirs, grown], axis=dim)
+        grown = jnp.where(here & reach == 0, mine_first, theirs_first)
+        reach = 2 * reach
+    return grown
 
 
 def with_halo(block, sides, width):
@@ -53,7 +65,7 @@
     mem_value = (value_base.reshape(-1, val_width).astype(jnp.float32) + embedded).astype(
         jnp.bfloat16
     )
-    queries = lax.all_gather(query_key, "mem", axis=0, tiled=True).reshape(-1, key_width)
+    queries = gather_by_bits(query_key, "mem", 0).reshape(-1, key_width)
     block_size = keys_local.shape[0]
     scores = jnp.dot(queries, keys_local.T, preferred_element_type=jnp.float32) * (
         1.0 / math.sqrt(key_width)

time: 155 us -> 150 us (0.968)
  blocking collectives: 78 us -> 58.9 us
  waiting for transfers between devices: 35.2 us -> 43.9 us
  starting transfers between devices: 7.7 us -> 12.1 us
    all_gather x1 -> x0, blocking collectives: 19.4 us -> none  [shards(): lax.all_gather(query_key, 'mem', axis=0, tiled=True).reshape(-1, key_width)]
    ppermute x0 -> x4, waiting for transfers between devices: none -> 8.77 us  [gather_by_bits(): theirs = lax.ppermute(grown, axis, [(d, d ^ reach) for d in range(ways)])]
    ppermute x0 -> x4, starting transfers between devices: none -> 4.41 us  [gather_by_bits(): theirs = lax.ppermute(grown, axis, [(d, d ^ reach) for d in range(ways)])]
  transfers between devices with their start and end apart: 3 -> 7, of which waited for: 2 -> 6; matrix products, arithmetic and copies ran while one was open for 1% -> 1% of each run, Pallas kernels for 0% -> 0%
where the time goes in v1:
time: 150 us; the launch traced here: 149 us
  blocking collectives  58.9 us (39%)
  waiting for transfers between devices  43.9 us (29%)
  matrix products  15.8 us (11%)
  between operations  14.3 us (10%)
  starting transfers between devices  12.1 us (8%)
  other arithmetic  2.57 us (2%)
    unnamed x1, blocking collectives  30.6 us
    reduce_scatter x1, waiting for transfers between devices, shards(): lax.psum_scatter(scaled_values, 'mem', scatter_dimension=0, tiled=True)  29.9 us
    pmax x1, blocking collectives, shards(): largest = lax.pmax(block_peak, 'mem')  28.3 us
    dot_general x8, matrix products, conv_taps(): jnp.dot(window, weight[row_step, col_step], preferred_element_type=jnp.fl...  10 us
    ppermute x4, waiting for transfers between devices, gather_by_bits(): theirs = lax.ppermute(grown, axis, [(d, d ^ reach) for d in range(ways)])  8.77 us
    ppermute x1, starting transfers between devices, with_halo(): lax.ppermute(lax.slice_in_dim(block, block.shape[dim] - width, None, axis...  5.75 us
    ppermute x1, waiting for transfers between devices, with_halo(): lax.ppermute(lax.slice_in_dim(block, 0, width, axis=dim), axis, backward)  5.25 us
    ppermute x4, starting transfers between devices, gather_by_bits(): theirs = lax.ppermute(grown, axis, [(d, d ^ reach) for d in range(ways)])  4.41 us
  transfers between devices with their start and end apart: 7, of which 6 were waited for; matrix products, arithmetic and copies ran while one was open for 1% of the time, Pallas kernels for 0%

profile of v1, /device:TPU:5, one launch (start us, length us, event | category | flops | bytes accessed | tf_op | source)
XLA Modules:
  0.0 149.0 jit_solution(10157949938138788741)
XLA Ops:
  6.5 0.0 copy-start
  6.5 0.0 reduce-scatter.2.cloned.1.call-start
  6.5 0.7 collective-permute-start
  7.2 1.0 collective-permute-done
  8.3 0.8 maximum_select_fusion.3
  9.1 0.0 collective-permute-start.1
  9.1 2.8 %collective-permute-done.1 = bf16[2,64,128]{2,1,0:T(8,128)(2,1)S(1)} collective-permute-done((bf16[2,64,128]{2,1,0:T(8,128)(2,1)S(1)}, bf16[2,64,128]{2,1,0:T(8,128)(2,1)S(1)}, u32[]{:S(2)}, u32[]{:S(2)}) %collective-permute-start.1) | collective-permute-done | bytes 32800 | tf_op jit(solution)/shard_map/ppermute | solution.py:12
  11.8 1.4 collective-permute-start.2
  13.2 1.8 %collective-permute-done.2 = bf16[4,64,128]{2,1,0:T(8,128)(2,1)S(1)} collective-permute-done((bf16[4,64,128]{2,1,0:T(8,128)(2,1)S(1)}, bf16[4,64,128]{2,1,0:T(8,128)(2,1)S(1)}, u32[]{:S(2)}, u32[]{:S(2)}) %collective-permute-start.2) | collective-permute-done | bytes 65568 | tf_op jit(solution)/shard_map/ppermute | solution.py:12
  15.0 2.4 %collective-permute-start.3 = (bf16[8,64,128]{2,1,0:T(8,128)(2,1)S(1)}, bf16[8,64,128]{2,1,0:T(8,128)(2,1)S(1)}, u32[]{:S(2)}, u32[]{:S(2)}) collective-permute-start(bf16[8,64,128]{2,1,0:T(8,128)(2,1)S(1)} %maximum_select_fusion.1), channel_id=1, source_target_pairs={{0,8},{1,9},{2,10},{3,11},{4,12},{5,13},{6,14},{7,15},{8,0},{9,1},... | collective-permute-start | bytes 393224 | tf_op jit(solution)/shard_map/ppermute | solution.py:12
  18.1 3.1 %collective-permute-done.3 = bf16[8,64,128]{2,1,0:T(8,128)(2,1)S(1)} collective-permute-done((bf16[8,64,128]{2,1,0:T(8,128)(2,1)S(1)}, bf16[8,64,128]{2,1,0:T(8,128)(2,1)S(1)}, u32[]{:S(2)}, u32[]{:S(2)}) %collective-permute-start.3) | collective-permute-done | bytes 131104 | tf_op jit(solution)/shard_map/ppermute | solution.py:12
  21.3 0.0 copy-done
  21.3 0.4 fusion
  21.7 0.0 copy-start.3
  21.7 0.0 copy-start.4
  21.8 28.3 %pmax.7 = f32[1024]{0:T(1024)S(1)} all-reduce(f32[1024]{0:T(1024)S(1)} %get-tuple-element.9), channel_id=1, replica_groups=mesh['groups'=2,'mem'=16] {'mem'}, use_global_device_ids=true, to_apply=%region_1.2 | all-reduce | flops 1024 | bytes 8192 | tf_op jit(solution)/shard_map/pmax | solution.py:82
  50.1 0.6 convert_reduce_fusion
  50.7 0.0 copy-done.3
  50.7 0.0 copy-done.4
  50.7 0.0 copy-start.5
  50.7 3.4 %convolution_multiply_fusion = f32[1024,512]{1,0:T(8,128)} fusion(bf16[1024,512]{0,1:T(8,128)(2,1)S(1)} %get-tuple-element.8, bf16[8,512]{1,0:T(8,128)(2,1)S(1)} %copy-done.3, bf16[512,512]{1,0:T(8,128)(2,1)} %bitcast.77, f32[1024]{0:T(1024)S(1)} %get-tuple-element.6, s32[512]{0:T(512)S(1)} %bitcast.78), kind=kOutput, calls=%fused_computation.4 | convolution fusion | flops 542380032 | bytes 3684352 | tf_op jit(solution)/shard_map/dot_general | solution.py:78
  54.1 0.0 copy-start.1
  54.1 0.0 reduce-scatter.2.cloned.1.call-update
  54.1 0.0 copy-done.5
  54.1 0.6 dynamic-slice
  54.7 0.1 reshape.73
  54.8 30.6 %all-reduce.1 = f32[16,64]{1,0:T(8,128)S(1)} all-reduce(f32[16,64]{1,0:T(8,128)S(1)} %reshape.73), channel_id=3, replica_groups=mesh['groups'=2,'mem'=16] {'mem'}, use_global_device_ids=true, to_apply=%region_4.5.clone | all-reduce | flops 1024 | bytes 8192
  85.4 0.7 dynamic-slice_bitcast_fusion
  86.1 29.9 %reduce-scatter.2.cloned.1.call-done = f32[1,64,512]{2,1,0:T(8,128)} async-done(((f32[16,64,512]{2,1,0:T(8,128)}), f32[1,64,512]{2,1,0:T(8,128)}) %reduce-scatter.2.cloned.1.call-update) | async-done | bytes 131088 | tf_op jit(solution)/shard_map/reduce_scatter | solution.py:88
  116.0 1.0 divide_convert_fusion
  116.9 0.0 copy-done.1
  117.0 5.7 %collective-permute-start.4 = (bf16[1,64,1024]{2,1,0:T(8,128)(2,1)S(1)}, bf16[1,64,1024]{2,1,0:T(8,128)(2,1)S(1)}, u32[]{:S(2)}, u32[]{:S(2)}) collective-permute-start(bf16[1,64,1024]{2,1,0:T(8,128)(2,1)S(1)} %pad_maximum_fusion), channel_id=1, source_target_pairs={{0,1},{1,2},{2,3},{3,4},{4,5},{5,6},{6,7},{7,8},{8,9},{9,10},{10,1... | collective-permute-start | bytes 393224 | tf_op jit(solution)/shard_map/ppermute | solution.py:25
  122.7 1.9 %collective-permute-start.5 = (bf16[1,64,1024]{2,1,0:T(8,128)(2,1)S(1)}, bf16[1,64,1024]{2,1,0:T(8,128)(2,1)S(1)}, u32[]{:S(2)}, u32[]{:S(2)}) collective-permute-start(bf16[1,64,1024]{2,1,0:T(8,128)(2,1)S(1)} %pad_maximum_fusion), channel_id=1, source_target_pairs={{1,0},{2,1},{3,2},{4,3},{5,4},{6,5},{7,6},{8,7},{9,8},{10,9},{11,1... | collective-permute-start | bytes 393224 | tf_op jit(solution)/shard_map/ppermute | solution.py:28
  124.7 0.0 collective-permute-done.4
  124.7 5.2 %collective-permute-done.5 = bf16[1,64,1024]{2,1,0:T(8,128)(2,1)S(1)} collective-permute-done((bf16[1,64,1024]{2,1,0:T(8,128)(2,1)S(1)}, bf16[1,64,1024]{2,1,0:T(8,128)(2,1)S(1)}, u32[]{:S(2)}, u32[]{:S(2)}) %collective-permute-start.5) | collective-permute-done | bytes 131104 | tf_op jit(solution)/shard_map/ppermute | solution.py:28
  129.9 0.1 select_maximum_fusion
  130.0 1.2 fusion.19
  131.3 1.2 fusion.9
  132.6 1.3 convolution_add_fusion.7
  133.8 0.0 copy-start.2
  133.8 1.3 convolution_add_fusion.6
  135.1 1.3 convolution_add_fusion.5
  136.4 1.3 convolution_add_fusion.4
  137.6 1.3 convolution_add_fusion.3
  138.9 1.3 convolution_add_fusion.2
  140.1 0.0 copy-done.2
  140.1 2.0 %fusion.6 = f32[1,64,8]{1,2,0:T(8,128)} fusion(bf16[256,8]{0,1:T(8,128)(2,1)S(1)} %copy-done.2, f32[64,256]{1,0:T(8,128)S(1)} %fusion.9, f32[64,256]{1,0:T(8,128)S(1)} %convolution_add_fusion.2, bf16[3,3,1024,256]{3,2,1,0:T(8,128)(2,1)} %param.16, bf16[1,64,1024]{2,1,0:T(8,128)(2,1)S(1)} %collective-permute-done.5), kind=kOutput, calls=%fused_computation.20 | convolution fusion | flops 33882112 | bytes 792576 | tf_op jit(solution)/shard_map/dot_general | solution.py:103
  (6 shorter events, 0.1 us)
Async XLA Ops:
  6.5 14.7 %copy-start = (bf16[4,128,128]{2,1,0:T(8,128)(2,1)S(1)}, bf16[4,128,128]{2,1,0:T(8,128)(2,1)}, u32[]{:S(2)}) copy-start(bf16[4,128,128]{2,1,0:T(8,128)(2,1)} %param.9) | copy-start | bytes 393220
  6.5 109.4 %reduce-scatter.2.cloned.1.call-start = ((), (), s32[]{:S(2)}) async-start(), calls=%async_computation.1 | async-start | bytes 2228224 | tf_op jit(solution)/shard_map/reduce_scatter | solution.py:88
  6.5 1.7 %collective-permute-start = (bf16[1,64,128]{2,1,0:T(8,128)(2,1)}, bf16[1,64,128]{2,1,0:T(8,128)(2,1)S(1)}, u32[]{:S(2)}, u32[]{:S(2)}) collective-permute-start(bf16[1,64,128]{2,1,0:T(8,128)(2,1)} %param.13), channel_id=1, source_target_pairs={{0,1},{1,0},{2,3},{3,2},{4,5},{5,4},{6,7},{7,6},{8,9},{9,8},{10,11... | collective-permute-start | bytes 49160 | tf_op jit(solution)/shard_map/ppermute | solution.py:12
  9.1 2.8 %collective-permute-start.1 = (bf16[2,64,128]{2,1,0:T(8,128)(2,1)S(1)}, bf16[2,64,128]{2,1,0:T(8,128)(2,1)S(1)}, u32[]{:S(2)}, u32[]{:S(2)}) collective-permute-start(bf16[2,64,128]{2,1,0:T(8,128)(2,1)S(1)} %maximum_select_fusion.3), channel_id=1, source_target_pairs={{0,2},{1,3},{2,0},{3,1},{4,6},{5,7},{6,4},{7,5},{8,10},{9,11},{10,... | collective-permute-start | bytes 98312 | tf_op jit(solution)/shard_map/ppermute | solution.py:12
  11.8 3.2 %collective-permute-start.2 = (bf16[4,64,128]{2,1,0:T(8,128)(2,1)S(1)}, bf16[4,64,128]{2,1,0:T(8,128)(2,1)S(1)}, u32[]{:S(2)}, u32[]{:S(2)}) collective-permute-start(bf16[4,64,128]{2,1,0:T(8,128)(2,1)S(1)} %maximum_select_fusion.2), channel_id=1, source_target_pairs={{0,4},{1,5},{2,6},{3,7},{4,0},{5,1},{6,2},{7,3},{8,12},{9,13},{10,... | collective-permute-start | bytes 196616 | tf_op jit(solution)/shard_map/ppermute | solution.py:12
  15.0 6.2 %collective-permute-start.3 = (bf16[8,64,128]{2,1,0:T(8,128)(2,1)S(1)}, bf16[8,64,128]{2,1,0:T(8,128)(2,1)S(1)}, u32[]{:S(2)}, u32[]{:S(2)}) collective-permute-start(bf16[8,64,128]{2,1,0:T(8,128)(2,1)S(1)} %maximum_select_fusion.1), channel_id=1, source_target_pairs={{0,8},{1,9},{2,10},{3,11},{4,12},{5,13},{6,14},{7,15},{8,0},{9,1},... | collective-permute-start | bytes 393224 | tf_op jit(solution)/shard_map/ppermute | solution.py:12
  21.7 29.0 %copy-start.3 = (bf16[8,512]{1,0:T(8,128)(2,1)S(1)}, bf16[8,512]{1,0:T(8,128)(2,1)}, u32[]{:S(2)}) copy-start(bf16[8,512]{1,0:T(8,128)(2,1)} %param.15) | copy-start | bytes 24580
  21.7 29.0 %copy-start.4 = (s32[4,128]{1,0:T(4,128)S(1)}, s32[4,128]{1,0:T(4,128)}, u32[]{:S(2)}) copy-start(s32[4,128]{1,0:T(4,128)} %param.11) | copy-start | bytes 6148
  50.7 3.4 %copy-start.5 = (u32[32]{0:T(128)S(1)}, u32[32]{0:T(128)}, u32[]{:S(2)}) copy-start(u32[32]{0:T(128)} %constant.34) | copy-start | bytes 388
  54.1 62.9 %copy-start.1 = (bf16[1,64,512]{2,1,0:T(8,128)(2,1)S(1)}, bf16[1,64,512]{2,1,0:T(8,128)(2,1)}, u32[]{:S(2)}) copy-start(bf16[1,64,512]{2,1,0:T(8,128)(2,1)} %param.14) | copy-start | bytes 196612
  117.0 7.7 %collective-permute-start.4 = (bf16[1,64,1024]{2,1,0:T(8,128)(2,1)S(1)}, bf16[1,64,1024]{2,1,0:T(8,128)(2,1)S(1)}, u32[]{:S(2)}, u32[]{:S(2)}) collective-permute-start(bf16[1,64,1024]{2,1,0:T(8,128)(2,1)S(1)} %pad_maximum_fusion), channel_id=1, source_target_pairs={{0,1},{1,2},{2,3},{3,4},{4,5},{5,6},{6,7},{7,8},{8,9},{9,10},{10,1... | collective-permute-start | bytes 393224 | tf_op jit(solution)/shard_map/ppermute | solution.py:25
  122.7 7.2 %collective-permute-start.5 = (bf16[1,64,1024]{2,1,0:T(8,128)(2,1)S(1)}, bf16[1,64,1024]{2,1,0:T(8,128)(2,1)S(1)}, u32[]{:S(2)}, u32[]{:S(2)}) collective-permute-start(bf16[1,64,1024]{2,1,0:T(8,128)(2,1)S(1)} %pad_maximum_fusion), channel_id=1, source_target_pairs={{1,0},{2,1},{3,2},{4,3},{5,4},{6,5},{7,6},{8,7},{9,8},{10,9},{11,1... | collective-permute-start | bytes 393224 | tf_op jit(solution)/shard_map/ppermute | solution.py:28
  133.8 6.3 %copy-start.2 = (bf16[256,8]{0,1:T(8,128)(2,1)S(1)}, bf16[256,8]{0,1:T(8,128)(2,1)}, u32[]{:S(2)}) copy-start(bf16[256,8]{0,1:T(8,128)(2,1)} %param.17) | copy-start | bytes 12292
Sparse Core Ops, SparseCore 0:
  54.2 61.6 reduce-scatter.1
